TPU v7x, 32 devices: a whole 2x2x4 slice. The times are simulated.
32 devices in a mesh: replica: 16 (over z, x, core), shard: 2 (over y).
Axes of the slice: x: 2, y: 2, z: 4, core: 2. Of those that a mesh axis runs over, the one named last changes fastest.
Arguments:
- latents: bfloat16 [32, 1024, 1152], P('replica', 'shard'), may hold values from -6 to 6
- conditions: bfloat16 [32, 1152], P('replica'), may hold values from -6 to 6
- cotangent: bfloat16 [32, 1024, 1152], P('replica', 'shard'), may hold values from -6 to 6
- counts: int32 [16], P('replica'), may hold values from 1 to 2, as said below
- w_ada: bfloat16 [1152, 6912], P('shard'), may hold values from -0.1875 to 0.1875
- b_ada: bfloat16 [6912], P('shard'), may hold values from -3 to 3
- w_qkv: bfloat16 [1152, 3456], P('shard'), may hold values from -0.1875 to 0.1875
- b_qv: bfloat16 [2304], P('shard'), may hold values from -3 to 3
- w_proj: bfloat16 [1152, 1152], P('shard'), may hold values from -3.5 to 3.5
- b_proj: bfloat16 [1152], P('shard'), may hold values from -3 to 3
- w_fc1: bfloat16 [1152, 4608], P('shard'), may hold values from -0.1875 to 0.1875
- b_fc1: bfloat16 [4608], P('shard'), may hold values from -3 to 3
- w_fc2: bfloat16 [4608, 1152], P('shard'), may hold values from -0.09375 to 0.09375
- b_fc2: bfloat16 [1152], P('shard'), may hold values from -3 to 3
Outputs:
- output: bfloat16 [32, 1024, 1152], P('replica', 'shard')
- grad_latents: float32 [32, 1024, 1152], P('replica', 'shard')
- grad_conditions: float32 [32, 1152], P('replica')
- grad_w_ada: float32 [1152, 6912], P('shard')
- grad_b_ada: float32 [6912], P('shard')
- grad_w_qkv: float32 [1152, 3456], P('shard')
- grad_b_qv: float32 [2304], P('shard')
- grad_w_proj: float32 [1152, 1152], P('shard')
- grad_b_proj: float32 [1152], P('shard')
- grad_w_fc1: float32 [1152, 4608], P('shard')
- grad_b_fc1: float32 [4608], P('shard')
- grad_w_fc2: float32 [4608, 1152], P('shard')
- grad_b_fc2: float32 [1152], P('shard')
Inputs may be any that keep to these rules, and one draw needn't show every extreme that they name: counts[r] live slots on replica r are its slots 0 to counts[r] - 1 of 2; some replica has all 2 live.
All inputs are finite; a program needn't handle non-finite values.
Results may differ from a plain program's by a relative error of at most 0.019.
Values may be sent and summed in bfloat16 or wider, within the bound.
A program may use at most 512 MiB of HBM per device.

v0:
```python
from functools import partial
import math
import jax
import jax.numpy as jnp
from jax import lax
from jax.sharding import PartitionSpec as P

HEADS = 16
HDIM = 72
epsilon = 1e-06


def layer_stats(values):
    centered = values - jnp.mean(values, axis=-1, keepdims=True)
    inverse = lax.rsqrt(jnp.mean(centered * centered, axis=-1, keepdims=True) + epsilon)
    return (centered * inverse, inverse)


def layer_back(normal, inverse, d_normal):
    first_mean = jnp.mean(d_normal, axis=-1, keepdims=True)
    second_mean = jnp.mean(d_normal * normal, axis=-1, keepdims=True)
    return inverse * (d_normal - first_mean - normal * second_mean)


def contract_last(left, right):
    return lax.dot_general(
        left, right, (((1,), (1,)), ((), ())), preferred_element_type=jnp.float32
    )


def forward_product(inputs, whole_pair):
    return (
        jnp.dot(inputs, whole_pair[0], preferred_element_type=jnp.float32),
        whole_pair[1].astype(jnp.float32),
    )


def backward_product(grads, whole_pair):
    return contract_last(grads, whole_pair[0])


def swap_cores(values):
    return lax.ppermute(values, "core", [(0, 1), (1, 0)])


def join_cores(mine, axis):
    theirs = swap_cores(mine)
    first = lax.axis_index("core") == 0
    return jnp.stack([jnp.where(first, mine, theirs), jnp.where(first, theirs, mine)], axis=axis)


def gather_rows(weight):
    rows, columns = weight.shape
    cores = lax.axis_size("core")
    part = rows // cores
    mine = lax.dynamic_slice_in_dim(weight, lax.axis_index("core") * part, part, 0)
    pieces = lax.all_gather(mine, "shard", axis=0, tiled=False)
    whole = join_cores(pieces, 1)
    return whole.reshape(rows * lax.axis_size("shard"), columns)


def weight_grad(inputs, grads, after):
    n_shard, n_core = (lax.axis_size("shard"), lax.axis_size("core"))
    terms = lax.dot_general(
        inputs, grads, (((0,), (0,)), ((), ())), preferred_element_type=jnp.float32
    ).astype(jnp.bfloat16)
    rows, columns = terms.shape
    part = rows // (n_shard * n_core)
    terms = terms.reshape(n_shard, n_core, part, columns)
    core = lax.axis_index("core")
    keep = lax.dynamic_index_in_dim(terms, core, 1, keepdims=False)
    send = lax.dynamic_index_in_dim(terms, 1 - core, 1, keepdims=False)
    terms = (keep.astype(jnp.float32) + swap_cores(send).astype(jnp.float32)).astype(jnp.bfloat16)
    terms = lax.psum_scatter(terms, "shard", scatter_dimension=0, tiled=True)
    terms = terms.reshape(part, columns)
    if after is not None:
        terms, _ = lax.optimization_barrier((terms, after))
    total = lax.psum(terms, "chip")
    return total


def finish_grad(total):
    joined = join_cores(total, 0).astype(jnp.float32)
    return joined.reshape(2 * total.shape[0], total.shape[1])


def shards(
    latents,
    conditions,
    cotangent,
    counts,
    w_ada,
    b_ada,
    w_qkv,
    b_qv,
    w_proj,
    b_proj,
    w_fc1,
    b_fc1,
    w_fc2,
    b_fc2,
):
    slots, block, width = latents.shape
    n_rows = slots * block
    scale = 1.0 / math.sqrt(HDIM)
    live = (jnp.arange(slots, dtype=jnp.int32) < counts[0]).astype(jnp.float32)[:, None, None]
    index = lax.axis_index("shard")
    biases = (b_ada, b_qv, b_proj, b_fc1, b_fc2)
    bias_all = lax.all_gather(jnp.concatenate(biases), "shard", axis=0, tiled=False)
    full_bias = []
    start = 0
    for bias in biases:
        size = bias.shape[0]
        full_bias.append(bias_all[:, start : start + size].reshape(-1))
        start += size
    full_qkv = (gather_rows(w_qkv), full_bias[1])
    full_proj = (gather_rows(w_proj), full_bias[2])
    full_fc1 = (gather_rows(w_fc1), full_bias[3])
    full_fc2 = (gather_rows(w_fc2), full_bias[4])
    cond_float = conditions.astype(jnp.float32)
    cond_act = jax.nn.silu(cond_float).astype(jnp.bfloat16)
    ada_rows = w_ada.shape[0]
    ada_length = b_ada.shape[0]
    own_cond = lax.dynamic_slice_in_dim(cond_act, index * ada_rows, ada_rows, 1)
    ada_part = jnp.dot(own_cond, w_ada, preferred_element_type=jnp.float32)
    modul = lax.psum(ada_part, "shard") + full_bias[0].astype(jnp.float32)
    shift_a, scale_a, gate_a, shift_m, scale_m, gate_m = [
        piece[:, None, :] for piece in jnp.split(modul, 6, axis=1)
    ]
    tokens = latents.astype(jnp.float32)
    norm_a, inv_a = layer_stats(tokens)
    normed = (norm_a * (1.0 + scale_a) + shift_a).astype(jnp.bfloat16).reshape(n_rows, width)
    qkv_prod, qv_bias = forward_product(normed, full_qkv)
    query = (
        (qkv_prod[:, :width] + qv_bias[:width])
        .astype(jnp.bfloat16)
        .reshape(slots, block, HEADS, HDIM)
    )
    keys_own = qkv_prod[:, width : 2 * width].astype(jnp.bfloat16).reshape(slots, block, width)
    values_own = (
        (qkv_prod[:, 2 * width :] + qv_bias[width:])
        .astype(jnp.bfloat16)
        .reshape(slots, block, width)
    )
    keys_all, values_all = (
        lax.all_gather(keys_own, "shard", axis=1, tiled=True),
        lax.all_gather(values_own, "shard", axis=1, tiled=True),
    )
    length = keys_all.shape[1]
    keys_h = keys_all.reshape(slots, length, HEADS, HDIM)
    values_h = values_all.reshape(slots, length, HEADS, HDIM)
    scores = (
        jnp.einsum("sqhd,skhd->shqk", query, keys_h, preferred_element_type=jnp.float32) * scale
    )
    top_score = jnp.max(scores, axis=-1, keepdims=True)
    log_total = top_score + jnp.log(jnp.sum(jnp.exp(scores - top_score), axis=-1, keepdims=True))
    probs_low = jnp.exp(scores - log_total).astype(jnp.bfloat16)
    attended = jnp.einsum(
        "shqk,skhd->sqhd", probs_low, values_h, preferred_element_type=jnp.float32
    )
    attended_wide = attended
    attended = attended.astype(jnp.bfloat16).reshape(n_rows, width)
    proj_prod, proj_bias = forward_product(attended, full_proj)
    branch_a = (proj_prod + proj_bias).reshape(slots, block, width)
    resid = tokens + gate_a * branch_a
    norm_m, inv_m = layer_stats(resid)
    mixed = (norm_m * (1.0 + scale_m) + shift_m).astype(jnp.bfloat16).reshape(n_rows, width)
    fc1_prod, fc1_bias = forward_product(mixed, full_fc1)
    activated, gelu_back = jax.vjp(partial(jax.nn.gelu, approximate=True), fc1_prod + fc1_bias)
    hidden = activated.astype(jnp.bfloat16)
    fc2_prod, fc2_bias = forward_product(hidden, full_fc2)
    branch_m = (fc2_prod + fc2_bias).reshape(slots, block, width)
    final = resid + gate_m * branch_m
    output = (final * live).astype(jnp.bfloat16)
    d_out = cotangent.astype(jnp.float32) * live
    d_gate_m = jnp.sum(d_out * branch_m, axis=1)
    d_branch_m = (gate_m * d_out).astype(jnp.bfloat16).reshape(n_rows, width)
    sum_fc2 = weight_grad(hidden, d_branch_m, None)
    bias_fc2 = jnp.sum(d_branch_m, axis=0, dtype=jnp.float32)
    d_hidden = backward_product(d_branch_m, full_fc2)
    d_pre = gelu_back(d_hidden)[0].astype(jnp.bfloat16)
    sum_fc1 = weight_grad(mixed, d_pre, sum_fc2)
    bias_fc1 = jnp.sum(d_pre, axis=0, dtype=jnp.float32)
    d_mixed = backward_product(d_pre, full_fc1).reshape(slots, block, width)
    d_shift_m = jnp.sum(d_mixed, axis=1)
    d_scale_m = jnp.sum(d_mixed * norm_m, axis=1)
    d_resid = d_out + layer_back(norm_m, inv_m, d_mixed * (1.0 + scale_m))
    d_gate_a = jnp.sum(d_resid * branch_a, axis=1)
    d_branch_a = (gate_a * d_resid).astype(jnp.bfloat16).reshape(n_rows, width)
    sum_proj = weight_grad(attended, d_branch_a, sum_fc1)
    bias_proj = jnp.sum(d_branch_a, axis=0, dtype=jnp.float32)
    d_attended = (
        backward_product(d_branch_a, full_proj)
        .astype(jnp.bfloat16)
        .reshape(slots, block, HEADS, HDIM)
    )
    scores = (
        jnp.einsum("sqhd,skhd->shqk", query, keys_h, preferred_element_type=jnp.float32) * scale
    )
    probs = jnp.exp(scores - log_total)
    d_probs = jnp.einsum(
        "sqhd,skhd->shqk", d_attended, values_h, preferred_element_type=jnp.float32
    )
    inner = jnp.sum(d_attended.astype(jnp.float32) * attended_wide, axis=-1)
    inner = jnp.swapaxes(inner, 1, 2)[..., None]
    d_scores = (probs * (d_probs - inner)).astype(jnp.bfloat16)
    d_query = (
        (
            jnp.einsum("shqk,skhd->sqhd", d_scores, keys_h, preferred_element_type=jnp.float32)
            * scale
        )
        .astype(jnp.bfloat16)
        .reshape(n_rows, width)
    )
    key_terms = (
        jnp.einsum("shqk,sqhd->skhd", d_scores, query, preferred_element_type=jnp.float32).reshape(
            slots, length, width
        )
        * scale
    )
    value_terms = jnp.einsum(
        "shqk,sqhd->skhd",
        probs.astype(jnp.bfloat16),
        d_attended,
        preferred_element_type=jnp.float32,
    ).reshape(slots, length, width)
    d_keys, d_values = (
        lax.psum_scatter(
            key_terms.astype(jnp.bfloat16), "shard", scatter_dimension=1, tiled=True
        ).astype(jnp.float32),
        lax.psum_scatter(
            value_terms.astype(jnp.bfloat16), "shard", scatter_dimension=1, tiled=True
        ).astype(jnp.float32),
    )
    d_keys = d_keys.astype(jnp.bfloat16).reshape(n_rows, width)
    d_values = d_values.astype(jnp.bfloat16).reshape(n_rows, width)
    d_qkv = jnp.concatenate([d_query, d_keys, d_values], axis=1)
    qv_terms = jnp.concatenate(
        [jnp.sum(d_query, axis=0, dtype=jnp.float32), jnp.sum(d_values, axis=0, dtype=jnp.float32)]
    )
    sum_qkv = weight_grad(normed, d_qkv, sum_proj)
    d_normed = backward_product(d_qkv, full_qkv).reshape(slots, block, width)
    d_shift_a = jnp.sum(d_normed, axis=1)
    d_scale_a = jnp.sum(d_normed * norm_a, axis=1)
    grad_latents = d_resid + layer_back(norm_a, inv_a, d_normed * (1.0 + scale_a))
    d_modul_part = jnp.concatenate(
        [d_shift_a, d_scale_a, d_gate_a, d_shift_m, d_scale_m, d_gate_m], axis=1
    )
    d_modul = lax.psum(d_modul_part, "shard").astype(jnp.bfloat16)
    cond_all = lax.all_gather(own_cond, ("chip", "core"), axis=0, tiled=True)
    d_modul_all = lax.all_gather(d_modul, ("chip", "core"), axis=0, tiled=True)
    grad_w_ada = lax.dot_general(
        cond_all, d_modul_all, (((0,), (0,)), ((), ())), preferred_element_type=jnp.float32
    )
    grad_b_ada = lax.dynamic_slice_in_dim(
        jnp.sum(d_modul_all, axis=0, dtype=jnp.float32), index * ada_length, ada_length, 0
    )
    d_cond_act = lax.all_gather(contract_last(d_modul, w_ada), "shard", axis=1, tiled=True)
    _, silu_back = jax.vjp(jax.nn.silu, cond_float)
    grad_conditions = silu_back(d_cond_act)[0]
    bias_terms = lax.psum(
        jnp.concatenate([qv_terms, bias_proj, bias_fc1, bias_fc2]), ("chip", "core", "shard")
    )
    bias_grads = []
    start = 0
    for bias in biases[1:]:
        size = bias.shape[0]
        bias_grads.append(lax.dynamic_slice_in_dim(bias_terms, start + index * size, size, 0))
        start += size * lax.axis_size("shard")
    return (
        output,
        grad_latents,
        grad_conditions,
        grad_w_ada,
        grad_b_ada,
        finish_grad(sum_qkv),
        bias_grads[0],
        finish_grad(sum_proj),
        bias_grads[1],
        finish_grad(sum_fc1),
        bias_grads[2],
        finish_grad(sum_fc2),
        bias_grads[3],
    )


def solution(mesh):
    names = mesh.axis_names
    n_replica, n_shard = (mesh.shape["replica"], mesh.shape["shard"])
    devices = mesh.devices.transpose(names.index("replica"), names.index("shard"))
    fine = jax.sharding.Mesh(devices.reshape(n_replica // 2, 2, n_shard), ("chip", "core", "shard"))
    placed = (
        P(("chip", "core"), "shard", None),
        P(("chip", "core"), None),
        P(("chip", "core"), "shard", None),
        P(("chip", "core")),
        P("shard", None),
        P("shard"),
        P("shard", None),
        P("shard"),
        P("shard", None),
        P("shard"),
        P("shard", None),
        P("shard"),
        P("shard", None),
        P("shard"),
    )
    return jax.shard_map(
        shards,
        mesh=fine,
        in_specs=placed,
        out_specs=(
            P(("chip", "core"), "shard", None),
            P(("chip", "core"), "shard", None),
            P(("chip", "core"), None),
            P("shard", None),
            P("shard"),
            P("shard", None),
            P("shard"),
            P("shard", None),
            P("shard"),
            P("shard", None),
            P("shard"),
            P("shard", None),
            P("shard"),
        ),
        check_vma=False,
    )
```

profile of v0, /device:TPU:1, one launch (start us, length us, event | category | flops | bytes accessed | tf_op | source)
XLA Modules:
  0.0 1356.5 jit_solution(5749713630772943146)
XLA Ops:
  22.9 44.0 %all-gather.20.cloned.1.call-done = bf16[576,3456]{1,0:T(8,128)(2,1)} async-done(((bf16[288,3456]{1,0:T(8,128)(2,1)}), bf16[576,3456]{1,0:T(8,128)(2,1)}) %all-gather.20.cloned.1.call-update) | async-done | bytes 3981328 | tf_op jit(solution)/shard_map/all_gather | solution.py:57
  67.6 4.4 fusion.59
  72.0 6.0 psum.49
  84.5 5.1 convert_reduce_fusion.2
  89.6 49.3 %all-gather.26.cloned.1.call-done = bf16[2304,1152]{1,0:T(8,128)(2,1)} async-done(((bf16[1152,1152]{1,0:T(8,128)(2,1)}), bf16[2304,1152]{1,0:T(8,128)(2,1)}) %all-gather.26.cloned.1.call-update) | async-done | bytes 5308432 | tf_op jit(solution)/shard_map/all_gather | solution.py:57
  139.6 5.0 select_bitcast_fusion.5
  144.6 6.3 pad_maximum_fusion.2
  150.9 12.3 fusion.60
  163.2 5.3 copy-done.8
  176.3 60.5 %all-gather.24.cloned.1.call-done = bf16[576,4608]{1,0:T(8,128)(2,1)} async-done(((bf16[288,4608]{1,0:T(8,128)(2,1)}), bf16[576,4608]{1,0:T(8,128)(2,1)}) %all-gather.24.cloned.1.call-update) | async-done | bytes 5308432 | tf_op jit(solution)/shard_map/all_gather | solution.py:57
  239.3 6.8 fusion.40
  246.1 9.6 reshape.308
  255.8 7.1 copy.62
  263.0 9.2 select_bitcast_fusion.1
  272.2 9.9 pad_maximum_fusion.1
  282.1 8.9 select_bitcast_fusion.3
  291.0 9.3 pad_maximum_fusion
  300.9 6.6 copy.61
  307.6 27.5 %multiply_reduce_fusion = (f32[2,16,512]{2,1,0:T(8,128)S(1)}, f32[2,16,512,1024]{3,2,1,0:T(8,128)}) fusion(bf16[2,512,16,72]{1,3,2,0:T(8,128)(2,1)} %copy.62, bf16[2,1024,16,72]{1,3,2,0:T(8,128)(2,1)} %bitcast.194), kind=kOutput, calls=%fused_computation.4 | convolution fusion | flops 2449457152 | bytes 74252288 | tf_op jit(solution)/shard_map/sqhd,skhd->shqk/dot_general | solution.py:153
  335.1 21.3 %exponential_reduce_fusion = f32[2,16,512]{2,1,0:T(8,128)S(1)} fusion(f32[2,16,512,1024]{3,2,1,0:T(8,128)} %get-tuple-element.71, f32[2,16,512]{2,1,0:T(8,128)S(1)} %get-tuple-element.70), kind=kLoop, calls=%fused_computation.2 | loop fusion | flops 50315264 | bytes 67239936 | tf_op jit(solution)/shard_map/reduce_sum | solution.py:156
  356.4 8.6 all-gather.16.cloned.1.call-done
  365.0 6.6 copy.59
  371.6 28.2 %bitcast_convert_fusion.2 = (bf16[2,512,16,72]{1,3,2,0:T(8,128)(2,1)}, f32[2,16,72,512]{3,2,1,0:T(8,128)}) fusion(bf16[2,1024,16,72]{1,3,2,0:T(8,128)(2,1)} %bitcast.192, f32[2,16,512,1024]{3,2,1,0:T(8,128)} %get-tuple-element.71, f32[2,16,512]{2,1,0:T(8,128)S(1)} %log_add_fusion), kind=kOutput, calls=%fused_computation.77 | convolution fusion | flops 2467430400 | bytes 78970880 | tf_op jit(solution)/shard_map/shqk,skhd->sqhd/dot_general | solution.py:158
  416.2 15.3 %fusion.61 = f32[1024,4608]{1,0:T(8,128)} fusion(bf16[1024,1152]{1,0:T(8,128)(2,1)S(1)} %bitcast.238, bf16[1152,4608]{1,0:T(8,128)(2,1)S(1)} %bitcast.210), kind=kOutput, calls=%fused_computation.179 | convolution fusion | flops 10871635968 | bytes 31850496 | tf_op jit(solution)/shard_map/dot_general | solution.py:33
  431.6 22.7 %convolution_convert_fusion = bf16[4608,1152]{1,0:T(8,128)(2,1)} fusion(bf16[1024,1152]{1,0:T(8,128)(2,1)S(1)} %bitcast.236, f32[1024,4608]{1,0:T(8,128)} %fusion.61, f32[4608]{0:T(1024)S(1)} %reshape.282), kind=kOutput, calls=%fused_computation.7 | convolution fusion | flops 10924130304 | bytes 31868928 | tf_op jit(solution)/shard_map/dot_general | solution.py:64
  454.3 5.2 dynamic-slice_bitcast_fusion
  460.1 29.3 %convert_reduce_fusion = (f32[4608]{0:T(1024)}, bf16[1024,4608]{1,0:T(8,128)(2,1)}) fusion(f32[1024,4608]{1,0:T(8,128)} %fusion.61, f32[4608]{0:T(1024)S(1)} %reshape.282, bf16[1024,1152]{1,0:T(8,128)(2,1)S(1)} %bitcast.237, bf16[4608,1152]{1,0:T(8,128)(2,1)} %bitcast.205), kind=kOutput, calls=%fused_computation.16 | convolution fusion | flops 10980159488 | bytes 41324544 | tf_op jit(solution)/shard_map/dot_general | solution.py:26
  489.5 21.3 %multiply_reduce_fusion.2 = (f32[2,1152]{1,0:T(2,128)}, f32[2,512]{1,0:T(2,128)S(1)}, f32[2,512]{1,0:T(2,128)S(1)}, f32[2,1152]{1,0:T(2,128)}, f32[2,512,1152]{2,1,0:T(8,128)}) fusion(f32[2,512,1152]{2,1,0:T(8,128)} %copy-done.2, f32[2,512]{1,0:T(2,128)S(1)} %add_rsqrt_fusion, f32[2,512]{1,0:T(2,128)S(1)} %broadcast_multiply_fusion.4, ...), kind=kOutput, calls=%fused_computation.84 | convolution fusion | flops 10882246656 | bytes 29535232 | tf_op jit(solution)/shard_map/dot_general | solution.py:26
  510.8 7.7 fusion.8
  519.2 21.8 %convolution_add_fusion = f32[1024,1152]{1,0:T(8,128)S(1)} fusion(bf16[4608,1152]{1,0:T(8,128)(2,1)} %bitcast.206, f32[1152]{0:T(1024)S(1)} %copy-done.47, f32[1024,4608]{1,0:T(8,128)} %fusion.61, f32[4608]{0:T(1024)S(1)} %reshape.282), kind=kOutput, calls=%fused_computation.62 | convolution fusion | flops 10920001536 | bytes 34232832 | tf_op jit(solution)/shard_map/dot_general | solution.py:33
  541.1 8.8 convert_reduce_fusion.3
  551.4 4.8 convolution_convert_fusion.4
  556.2 9.6 reshape.309
  565.8 7.1 copy.68
  577.0 40.1 %multiply_convert_fusion = bf16[2,16,512,1024]{3,2,1,0:T(8,128)(2,1)} fusion(f32[2,16,512,1024]{3,2,1,0:T(8,128)} %get-tuple-element.71, f32[2,16,512]{2,1,0:T(8,128)S(1)} %bitcast.247, f32[2,16,512]{2,1,0:T(8,128)S(1)} %copy-done.12, bf16[2,512,16,72]{1,3,2,0:T(8,128)(2,1)S(1)} %copy-done.5, bf16[2,1024,16,72]{1,3,2,0:T(8,128)(2,1)} %bitcast.193), kind=kOutput, calls=%fused_computation | convolution fusion | flops 2499805184 | bytes 107872256 | tf_op jit(solution)/shard_map/sqhd,skhd->shqk/dot_general | solution.py:201
  617.2 19.4 %multiply_convert_fusion.2 = bf16[2,16,72,1024]{3,2,1,0:T(8,128)(2,1)} fusion(bf16[2,512,16,72]{1,3,2,0:T(8,128)(2,1)} %copy.62, bf16[2,16,512,1024]{3,2,1,0:T(8,128)(2,1)} %multiply_convert_fusion), kind=kOutput, calls=%fused_computation.25 | convolution fusion | flops 2420637696 | bytes 40632320 | tf_op jit(solution)/shard_map/shqk,sqhd->skhd/dot_general | solution.py:216
  636.6 6.7 copy.71
  643.4 28.0 %fusion.43 = bf16[2,16,72,1024]{3,2,1,0:T(8,128)(2,1)} fusion(bf16[2,512,16,72]{1,3,2,0:T(8,128)(2,1)} %copy.68, f32[2,16,512,1024]{3,2,1,0:T(8,128)} %get-tuple-element.71, f32[2,16,512]{2,1,0:T(8,128)S(1)} %copy-done.12), kind=kOutput, calls=%fused_computation.105 | convolution fusion | flops 2468610048 | bytes 74252288 | tf_op jit(solution)/shard_map/shqk,sqhd->skhd/dot_general | solution.py:221
  671.4 6.8 copy.73
  678.2 14.8 %convolution_convert_fusion.1 = bf16[1152,4608]{1,0:T(8,128)(2,1)S(1)} fusion(bf16[1024,1152]{1,0:T(8,128)(2,1)} %bitcast.239, bf16[1024,4608]{1,0:T(8,128)(2,1)} %get-tuple-element.32), kind=kOutput, calls=%fused_computation.8 | convolution fusion | flops 10876944384 | bytes 22413312 | tf_op jit(solution)/shard_map/dot_general | solution.py:64
  693.5 8.9 collective-permute-done.6
  702.3 6.2 fusion.9
  708.6 5.6 convolution_convert_fusion.3
  716.2 18.1 %convert_reduce_fusion.5 = (f32[16,72]{1,0:T(8,128)S(1)}, bf16[2,16,72,512]{3,2,1,0:T(8,128)(2,1)S(1)}) fusion(bf16[2,1024,16,72]{1,3,2,0:T(8,128)(2,1)} %bitcast.195, bf16[2,16,512,1024]{3,2,1,0:T(8,128)(2,1)} %multiply_convert_fusion), kind=kOutput, calls=%fused_computation.82 | convolution fusion | flops 2420636672 | bytes 40636928 | tf_op jit(solution)/shard_map/shqk,skhd->sqhd/dot_general | solution.py:209
  740.4 4.3 copy.77
  744.7 20.6 %reduce-scatter.9.cloned.1.call-done = bf16[2,512,1152]{2,1,0:T(8,128)(2,1)} async-done(((bf16[2,1024,1152]{2,1,0:T(8,128)(2,1)}), bf16[2,512,1152]{2,1,0:T(8,128)(2,1)}) %reduce-scatter.9.cloned.1.call-update) | async-done | bytes 2359312 | tf_op jit(solution)/shard_map/reduce_scatter | solution.py:231
  769.5 12.2 convolution_convert_fusion.2
  787.9 46.5 %reduce-scatter.15.cloned.1.call-done = bf16[1,288,4608]{2,1,0:T(8,128)(2,1)} async-done(((bf16[2,288,4608]{2,1,0:T(8,128)(2,1)}), bf16[1,288,4608]{2,1,0:T(8,128)(2,1)}) %reduce-scatter.15.cloned.1.call-update) | async-done | bytes 2654224 | tf_op jit(solution)/shard_map/reduce_scatter | solution.py:74
  834.4 118.8 %all-reduce.5.cloned.1.call-done = bf16[1152,1152]{1,0:T(8,128)(2,1)} async-done(((bf16[1152,1152]{1,0:T(8,128)(2,1)}), bf16[1152,1152]{1,0:T(8,128)(2,1)}) %all-reduce.5.cloned.1.call-update) | async-done | bytes 2654224 | tf_op jit(solution)/shard_map/psum | solution.py:78
  953.3 21.4 %all-gather.7 = bf16[16,2,576]{2,1,0:T(2,128)(2,1)S(1)} all-gather(bf16[1,2,576]{2,1,0:T(2,128)(2,1)S(1)} %bitcast.254), channel_id=1, replica_groups=mesh['chip'=8,'core'=2,'shard'=2] {'chip','core'}, dimensions={0}, use_global_device_ids=true | all-gather | bytes 39168 | tf_op jit(solution)/shard_map/all_gather | solution.py:250
  974.8 4.3 copy.74
  979.1 6.2 fusion.10
  987.6 17.0 %fusion.38 = (f32[2,1152]{1,0:T(2,128)S(1)}, f32[2,512]{1,0:T(2,128)S(1)}, f32[2,512]{1,0:T(2,128)S(1)}, f32[2,1152]{1,0:T(2,128)S(1)}, f32[2,512,1152]{2,1,0:T(8,128)}) fusion(bf16[2,512,1152]{2,1,0:T(8,128)(2,1)} %param.14, f32[2,512]{1,0:T(2,128)S(1)} %copy-done.38, f32[2,512]{1,0:T(2,128)S(1)} %copy-done.32, f32[2,1152]{1,0:T(2,128)S(1)} %copy-done.30, ...), kind=kOutput, calls=%fused_computation.69 | convolution fusion | flops 8186750976 | bytes 22162432 | tf_op jit(solution)/shard_map/dot_general | solution.py:26
  1004.7 7.9 multiply_reduce_fusion.3
  1012.8 37.0 %psum.55 = f32[9216]{0:T(1024)S(1)} all-reduce(f32[9216]{0:T(1024)S(1)} %constant_dynamic-update-slice_fusion.10), channel_id=1, replica_groups=mesh['chip'=8,'core'=2,'shard'=2] {'chip','core','shard'}, use_global_device_ids=true, to_apply=%region_35.36 | all-reduce | flops 9216 | bytes 73728 | tf_op jit(solution)/shard_map/psum | solution.py:261
  1051.2 8.4 psum.50
  1059.6 5.4 convolution_bitcast_fusion
  1068.3 27.5 %all-gather.8 = bf16[16,2,6912]{2,1,0:T(2,128)(2,1)S(1)} all-gather(bf16[1,2,6912]{2,1,0:T(2,128)(2,1)S(1)} %bitcast.249), channel_id=1, replica_groups=mesh['chip'=8,'core'=2,'shard'=2] {'chip','core'}, dimensions={0}, use_global_device_ids=true | all-gather | bytes 470016 | tf_op jit(solution)/shard_map/all_gather | solution.py:251
  1098.1 8.1 fusion.62
  1112.7 43.0 %reduce-scatter.11.cloned.1.call-done = bf16[1,288,3456]{2,1,0:T(8,128)(2,1)} async-done(((bf16[2,288,3456]{2,1,0:T(8,128)(2,1)}), bf16[1,288,3456]{2,1,0:T(8,128)(2,1)}) %reduce-scatter.11.cloned.1.call-update) | async-done | bytes 1990672 | tf_op jit(solution)/shard_map/reduce_scatter | solution.py:74
  1155.7 75.7 %all-reduce.9.cloned.1.call-done = bf16[288,1152]{1,0:T(8,128)(2,1)} async-done(((bf16[288,1152]{1,0:T(8,128)(2,1)}), bf16[288,1152]{1,0:T(8,128)(2,1)}) %all-reduce.9.cloned.1.call-update) | async-done | bytes 663568 | tf_op jit(solution)/shard_map/psum | solution.py:78
  1233.5 7.3 bitcast_convert_fusion
  1242.9 91.8 %all-reduce.11.cloned.1.call-done = bf16[288,3456]{1,0:T(8,128)(2,1)} async-done(((bf16[288,3456]{1,0:T(8,128)(2,1)}), bf16[288,3456]{1,0:T(8,128)(2,1)}) %all-reduce.11.cloned.1.call-update) | async-done | bytes 1990672 | tf_op jit(solution)/shard_map/psum | solution.py:78
  1339.0 5.9 bitcast_convert_fusion.1
  (261 shorter events, 104.8 us)
Async XLA Ops:
  7.2 6.8 copy-start
  7.2 59.7 %all-gather.20.cloned.1.call-start = ((), (), s32[]{:S(2)}) async-start(), calls=%async_computation.18 | async-start | bytes 5971968 | tf_op jit(solution)/shard_map/all_gather | solution.py:57
  10.3 128.6 %all-gather.26.cloned.1.call-start = ((), (), s32[]{:S(2)}) async-start(), calls=%async_computation.21 | async-start | bytes 7962624 | tf_op jit(solution)/shard_map/all_gather | solution.py:57
  13.9 4.7 copy-start.46
  13.9 4.7 copy-start.48
  13.9 4.7 copy-start.49
  13.9 4.7 copy-start.52
  13.9 4.6 copy-start.53
  14.0 156.5 %all-gather.22.cloned.1.call-start = ((), (), s32[]{:S(2)}) async-start(), calls=%async_computation.19 | async-start | bytes 1990656 | tf_op jit(solution)/shard_map/all_gather | solution.py:57
  14.9 221.9 %all-gather.24.cloned.1.call-start = ((), (), s32[]{:S(2)}) async-start(), calls=%async_computation.20 | async-start | bytes 7962624 | tf_op jit(solution)/shard_map/all_gather | solution.py:57
  18.4 282.5 %all-gather.18.cloned.1.call-start = ((), (), s32[]{:S(2)}) async-start(), calls=%async_computation.7 | async-start | bytes 7077888 | tf_op jit(solution)/shard_map/all_gather | solution.py:146
  22.9 44.7 %copy-start.39 = (bf16[2,576]{1,0:T(2,128)(2,1)}, bf16[2,576]{1,0:T(2,128)(2,1)S(1)}, u32[]{:S(2)}) copy-start(bf16[2,576]{1,0:T(2,128)(2,1)S(1)} %fusion.50) | copy-start | bytes 6916
  66.9 72.7 %collective-permute-start = (bf16[2,288,3456]{2,1,0:T(8,128)(2,1)}, bf16[2,288,3456]{2,1,0:T(8,128)(2,1)}, u32[]{:S(2)}, u32[]{:S(2)}) collective-permute-start(bf16[2,288,3456]{2,1,0:T(8,128)(2,1)} %bitcast.224), channel_id=1, source_target_pairs={{0,2},{2,0},{1,3},{3,1},{4,6},{6,4},{5,7},{7,5},{8,10},{10,8},{9,1... | collective-permute-start | bytes 11943944 | tf_op jit(solution)/shard_map/ppermute | solution.py:43
  80.6 9.0 copy-start.31
  83.9 5.7 copy-start.50
  83.9 5.7 copy-start.37
  84.5 5.1 copy-start.24
  84.5 5.1 copy-start.29
  84.5 323.9 %copy-start.27 = (f32[2,1152]{1,0:T(2,128)}, f32[2,1152]{1,0:T(2,128)S(1)}, u32[]{:S(2)}) copy-start(f32[2,1152]{1,0:T(2,128)S(1)} %get-tuple-element.65) | copy-start | bytes 27652
  138.9 124.0 %collective-permute-start.3 = (bf16[2,1152,1152]{2,1,0:T(8,128)(2,1)}, bf16[2,1152,1152]{2,1,0:T(8,128)(2,1)}, u32[]{:S(2)}, u32[]{:S(2)}) collective-permute-start(bf16[2,1152,1152]{2,1,0:T(8,128)(2,1)} %bitcast.220), channel_id=1, source_target_pairs={{0,2},{2,0},{1,3},{3,1},{4,6},{6,4},{5,7},{7,5},{8,10},{10,8},{9,1... | collective-permute-start | bytes 15925256 | tf_op jit(solution)/shard_map/ppermute | solution.py:43
  144.6 6.3 copy-start.18
  163.2 5.3 copy-start.8
  170.3 194.8 %all-gather.16.cloned.1.call-start = ((), (), s32[]{:S(2)}) async-start(), calls=%async_computation.6 | async-start | bytes 7077888 | tf_op jit(solution)/shard_map/all_gather | solution.py:147
  170.5 3.5 collective-permute-start.1
  236.9 45.2 %collective-permute-start.2 = (bf16[2,288,4608]{2,1,0:T(8,128)(2,1)}, bf16[2,288,4608]{2,1,0:T(8,128)(2,1)}, u32[]{:S(2)}, u32[]{:S(2)}) collective-permute-start(bf16[2,288,4608]{2,1,0:T(8,128)(2,1)} %bitcast.222), channel_id=1, source_target_pairs={{0,2},{2,0},{1,3},{3,1},{4,6},{6,4},{5,7},{7,5},{8,10},{10,8},{9,1... | collective-permute-start | bytes 15925256 | tf_op jit(solution)/shard_map/ppermute | solution.py:43
  262.9 453.2 %reduce-scatter.17.cloned.1.call-start = ((), (), s32[]{:S(2)}) async-start(), calls=%async_computation.13 | async-start | bytes 7962624 | tf_op jit(solution)/shard_map/reduce_scatter | solution.py:74
  356.4 15.2 %copy-start.11 = (f32[2,16,512]{2,1,0:T(8,128)}, f32[2,16,512]{2,1,0:T(8,128)S(1)}, u32[]{:S(2)}) copy-start(f32[2,16,512]{2,1,0:T(8,128)S(1)} %log_add_fusion) | copy-start | bytes 196612
  399.8 4.9 copy-start.13
  408.5 6.4 slice-start
  408.5 6.4 slice-start.1
  410.8 5.4 slice-start.2
  414.9 16.7 %copy-start.20 = (bf16[2,512,1152]{2,1,0:T(8,128)(2,1)}, bf16[2,512,1152]{2,1,0:T(8,128)(2,1)S(1)}, u32[]{:S(2)}) copy-start(bf16[2,512,1152]{2,1,0:T(8,128)(2,1)S(1)} %add_convert_fusion) | copy-start | bytes 7077892
  416.2 15.3 %copy-start.19 = (bf16[2,512,1152]{2,1,0:T(8,128)(2,1)S(1)}, bf16[2,512,1152]{2,1,0:T(8,128)(2,1)}, u32[]{:S(2)}) copy-start(bf16[2,512,1152]{2,1,0:T(8,128)(2,1)} %get-tuple-element.30) | copy-start | bytes 7077892
  459.5 51.3 %collective-permute-start.7 = (bf16[2,1152,1152]{2,1,0:T(8,128)(2,1)}, bf16[2,1152,1152]{2,1,0:T(8,128)(2,1)}, u32[]{:S(2)}, u32[]{:S(2)}) collective-permute-start(bf16[2,1152,1152]{2,1,0:T(8,128)(2,1)} %dynamic-slice_bitcast_fusion), channel_id=1, source_target_pairs={{0,2},{2,0},{1,3},{3,1},{4,6},{6,4},{5,7},{7,5},{8,10},{10,8},{9,1... | collective-permute-start | bytes 15925256 | tf_op jit(solution)/shard_map/ppermute | solution.py:43
  518.6 22.5 %copy-start.25 = (f32[2,1152]{1,0:T(2,128)S(1)}, f32[2,1152]{1,0:T(2,128)}, u32[]{:S(2)}) copy-start(f32[2,1152]{1,0:T(2,128)} %copy-done.24) | copy-start | bytes 27652
  518.6 22.5 %copy-start.28 = (f32[2,1152]{1,0:T(2,128)S(1)}, f32[2,1152]{1,0:T(2,128)}, u32[]{:S(2)}) copy-start(f32[2,1152]{1,0:T(2,128)} %copy-done.27) | copy-start | bytes 27652
  518.6 22.5 %copy-start.51 = (f32[2]{0:T(128)S(1)}, f32[2]{0:T(128)}, u32[]{:S(2)}) copy-start(f32[2]{0:T(128)} %copy-done.50) | copy-start | bytes 28
  518.6 221.8 %reduce-scatter.7.cloned.1.call-start = ((), (), s32[]{:S(2)}) async-start(), calls=%async_computation.8 | async-start | bytes 7077888 | tf_op jit(solution)/shard_map/reduce_scatter | solution.py:228
  519.2 21.9 %copy-start.9 = (bf16[2,512,1152]{2,1,0:T(8,128)(2,1)S(1)}, bf16[2,512,1152]{2,1,0:T(8,128)(2,1)}, u32[]{:S(2)}) copy-start(bf16[2,512,1152]{2,1,0:T(8,128)(2,1)} %param.16) | copy-start | bytes 7077892
  541.1 10.3 copy-start.14
  643.3 121.9 %reduce-scatter.9.cloned.1.call-start = ((), (), s32[]{:S(2)}) async-start(), calls=%async_computation.9 | async-start | bytes 7077888 | tf_op jit(solution)/shard_map/reduce_scatter | solution.py:231
  678.2 156.2 %reduce-scatter.15.cloned.1.call-start = ((), (), s32[]{:S(2)}) async-start(), calls=%async_computation.12 | async-start | bytes 7962624 | tf_op jit(solution)/shard_map/reduce_scatter | solution.py:74
  693.4 8.9 collective-permute-start.6
  708.6 244.6 %all-reduce.5.cloned.1.call-start = ((), (), s32[]{:S(2)}) async-start(), calls=%async_computation.14 | async-start | bytes 5308416 | tf_op jit(solution)/shard_map/psum | solution.py:78
  715.9 23.0 %collective-permute-start.5 = (bf16[2,288,1152]{2,1,0:T(8,128)(2,1)S(1)}, bf16[2,288,1152]{2,1,0:T(8,128)(2,1)S(1)}, u32[]{:S(2)}, u32[]{:S(2)}) collective-permute-start(bf16[2,288,1152]{2,1,0:T(8,128)(2,1)S(1)} %dynamic-slice_bitcast_fusion.3), channel_id=1, source_target_pairs={{0,2},{2,0},{1,3},{3,1},{4,6},{6,4},{5,7},{7,5},{8,10},{10,8},{9,1... | collective-permute-start | bytes 3981320 | tf_op jit(solution)/shard_map/ppermute | solution.py:43
  716.1 390.1 %reduce-scatter.13.cloned.1.call-start = ((), (), s32[]{:S(2)}) async-start(), calls=%async_computation.11 | async-start | bytes 1990656 | tf_op jit(solution)/shard_map/reduce_scatter | solution.py:74
  740.3 365.9 %all-reduce.7.cloned.1.call-start = ((), (), s32[]{:S(2)}) async-start(), calls=%async_computation.15 | async-start | bytes 5308416 | tf_op jit(solution)/shard_map/psum | solution.py:78
  785.0 168.3 %copy-start.40 = (bf16[2,576]{1,0:T(2,128)(2,1)S(1)}, bf16[2,576]{1,0:T(2,128)(2,1)}, u32[]{:S(2)}) copy-start(bf16[2,576]{1,0:T(2,128)(2,1)} %copy-done.39) | copy-start | bytes 6916
  787.2 191.9 %collective-permute-start.4 = (bf16[2,288,3456]{2,1,0:T(8,128)(2,1)}, bf16[2,288,3456]{2,1,0:T(8,128)(2,1)}, u32[]{:S(2)}, u32[]{:S(2)}) collective-permute-start(bf16[2,288,3456]{2,1,0:T(8,128)(2,1)} %dynamic-slice_bitcast_fusion.2), channel_id=1, source_target_pairs={{0,2},{2,0},{1,3},{3,1},{4,6},{6,4},{5,7},{7,5},{8,10},{10,8},{9,1... | collective-permute-start | bytes 11943944 | tf_op jit(solution)/shard_map/ppermute | solution.py:43
  953.2 202.4 %reduce-scatter.11.cloned.1.call-start = ((), (), s32[]{:S(2)}) async-start(), calls=%async_computation.10 | async-start | bytes 5971968 | tf_op jit(solution)/shard_map/reduce_scatter | solution.py:74
  985.4 246.0 %all-reduce.9.cloned.1.call-start = ((), (), s32[]{:S(2)}) async-start(), calls=%async_computation.16 | async-start | bytes 1327104 | tf_op jit(solution)/shard_map/psum | solution.py:78
  987.6 17.1 %copy-start.4 = (bf16[2,512,1152]{2,1,0:T(8,128)(2,1)S(1)}, bf16[2,512,1152]{2,1,0:T(8,128)(2,1)}, u32[]{:S(2)}) copy-start(bf16[2,512,1152]{2,1,0:T(8,128)(2,1)} %param.14) | copy-start | bytes 7077892
  1004.6 8.0 copy-start.45
  1004.7 8.1 copy-start.42
  1004.7 46.5 %copy-start.44 = (f32[2,1152]{1,0:T(2,128)S(1)}, f32[2,1152]{1,0:T(2,128)}, u32[]{:S(2)}) copy-start(f32[2,1152]{1,0:T(2,128)} %get-tuple-element.19) | copy-start | bytes 27652
  1004.7 46.5 %copy-start.35 = (f32[2,1152]{1,0:T(2,128)S(1)}, f32[2,1152]{1,0:T(2,128)}, u32[]{:S(2)}) copy-start(f32[2,1152]{1,0:T(2,128)} %get-tuple-element.57) | copy-start | bytes 27652
  1012.6 94.1 %collective-permute-start.11 = (bf16[1152,1152]{1,0:T(8,128)(2,1)}, bf16[1152,1152]{1,0:T(8,128)(2,1)}, u32[]{:S(2)}, u32[]{:S(2)}) collective-permute-start(bf16[1152,1152]{1,0:T(8,128)(2,1)} %all-reduce.5.cloned.1.call-done), channel_id=1, source_target_pairs={{0,2},{2,0},{1,3},{3,1},{4,6},{6,4},{5,7},{7,5},{8,10},{10,8},{9,1... | collective-permute-start | bytes 7962632 | tf_op jit(solution)/shard_map/ppermute | solution.py:43
  1059.6 37.9 %copy-start.34 = (bf16[2,1152]{1,0:T(2,128)(2,1)S(1)}, bf16[2,1152]{1,0:T(2,128)(2,1)}, u32[]{:S(2)}) copy-start(bf16[2,1152]{1,0:T(2,128)(2,1)} %param.15) | copy-start | bytes 13828
  1106.3 228.4 %all-reduce.11.cloned.1.call-start = ((), (), s32[]{:S(2)}) async-start(), calls=%async_computation.17 | async-start | bytes 3981312 | tf_op jit(solution)/shard_map/psum | solution.py:78
  1106.5 229.1 %collective-permute-start.10 = (bf16[288,4608]{1,0:T(8,128)(2,1)}, bf16[288,4608]{1,0:T(8,128)(2,1)}, u32[]{:S(2)}, u32[]{:S(2)}) collective-permute-start(bf16[288,4608]{1,0:T(8,128)(2,1)} %all-reduce.7.cloned.1.call-done), channel_id=1, source_target_pairs={{0,2},{2,0},{1,3},{3,1},{4,6},{6,4},{5,7},{7,5},{8,10},{10,8},{9,1... | collective-permute-start | bytes 7962632 | tf_op jit(solution)/shard_map/ppermute | solution.py:43
  1231.4 9.4 copy-start.23
  1231.4 9.4 collective-permute-start.9
  1334.7 10.2 collective-permute-start.8
  1339.0 5.9 copy-start.22
  (21 other events, 64.5 us)
Sparse Core Ops, SparseCore 0:
  10.5 56.4 all-gather.19
  69.0 69.8 all-gather.25
  141.1 24.4 all-gather.21
  167.5 69.2 all-gather.23
  238.2 62.6 all-gather.17
  302.3 62.6 all-gather.15
  518.7 65.8 reduce-scatter.16
  643.5 59.3 reduce-scatter.6
  705.2 59.9 reduce-scatter.8
  768.0 66.3 reduce-scatter.14
  838.1 115.0 all-reduce.4
  955.3 23.3 reduce-scatter.12
  982.8 117.3 all-reduce.6
  1103.0 52.5 reduce-scatter.10
  1159.3 72.0 all-reduce.8
  1234.9 99.7 all-reduce.10
where the time goes:
time: 1370 us; the launch traced here: 1360 us
  waiting for transfers between devices  571 us (42%)
  matrix products  360 us (26%)
  other arithmetic  169 us (12%)
  local copies, waits for them, and re-layouts  125 us (9%)
  blocking collectives  108 us (8%)
  between operations  15.9 us (1%)
    psum x4, waiting for transfers between devices, weight_grad(): total = lax.psum(terms, 'chip')  286 us
    all_gather x4, waiting for transfers between devices, gather_rows(): pieces = lax.all_gather(mine, 'shard', axis=0, tiled=False)  154 us
    reduce_scatter x4, waiting for transfers between devices, weight_grad(): terms = lax.psum_scatter(terms, 'shard', scatter_dimension=0, tiled=True)  89.5 us
    dot_general x5, matrix products, contract_last(): lax.dot_general(left, right, (((1,), (1,)), ((), ())), preferred_element_...  77.8 us
    another operation x16, other arithmetic, join_cores(): jnp.stack([jnp.where(first, mine, theirs), jnp.where(first, theirs, mine)...  63.1 us
    dot_general x4, matrix products, weight_grad(): lax.dot_general(inputs, grads, (((0,), (0,)), ((), ())), preferred_elemen...  55.3 us
    dot_general x4, matrix products, forward_product(): jnp.dot(inputs, whole_pair[0], preferred_element_type=jnp.float32)  53.1 us
    dot_general x1, matrix products, shards(): jnp.einsum('sqhd,skhd->shqk', d_attended, values_h, preferred_element_typ...  40.1 us
  transfers between devices with their start and end apart: 28, of which 13 were waited for; matrix products, arithmetic and copies ran while one was open for 39% of the time, Pallas kernels for 0%

commit v1 on v0

--- a/solution.py
+++ b/solution.py
@@ -259,7 +259,8 @@
     _, silu_back = jax.vjp(jax.nn.silu, cond_float)
     grad_conditions = silu_back(d_cond_act)[0]
     bias_terms = lax.psum(
-        jnp.concatenate([qv_terms, bias_proj, bias_fc1, bias_fc2]), ("chip", "core", "shard")
+        lax.psum(jnp.concatenate([qv_terms, bias_proj, bias_fc1, bias_fc2]), ("core", "shard")),
+        "chip",
     )
     bias_grads = []
     start = 0

time: 1370 us -> 1370 us (level)
    psum x1 -> x2, blocking collectives: 37 us -> 39.9 us  [the longest x1 26.8 us: shards(): lax.psum(lax.psum(jnp.concatenate([qv_terms, bias_proj, bias_fc1, bias_fc...]
where the time goes in v1:
time: 1370 us; the launch traced here: 1360 us
  waiting for transfers between devices  565 us (41%)
  matrix products  360 us (26%)
  other arithmetic  169 us (12%)
  local copies, waits for them, and re-layouts  125 us (9%)
  blocking collectives  115 us (8%)
  between operations  15.9 us (1%)
    psum x4, waiting for transfers between devices, weight_grad(): total = lax.psum(terms, 'chip')  286 us
    all_gather x4, waiting for transfers between devices, gather_rows(): pieces = lax.all_gather(mine, 'shard', axis=0, tiled=False)  154 us
    reduce_scatter x4, waiting for transfers between devices, weight_grad(): terms = lax.psum_scatter(terms, 'shard', scatter_dimension=0, tiled=True)  82.8 us
    dot_general x5, matrix products, contract_last(): lax.dot_general(left, right, (((1,), (1,)), ((), ())), preferred_element_...  77.8 us
    another operation x16, other arithmetic, join_cores(): jnp.stack([jnp.where(first, mine, theirs), jnp.where(first, theirs, mine)...  63 us
    dot_general x4, matrix products, weight_grad(): lax.dot_general(inputs, grads, (((0,), (0,)), ((), ())), preferred_elemen...  55.3 us
    dot_general x4, matrix products, forward_product(): jnp.dot(inputs, whole_pair[0], preferred_element_type=jnp.float32)  53.2 us
    dot_general x1, matrix products, shards(): jnp.einsum('sqhd,skhd->shqk', d_attended, values_h, preferred_element_typ...  40.1 us
  transfers between devices with their start and end apart: 28, of which 13 were waited for; matrix products, arithmetic and copies ran while one was open for 39% of the time, Pallas kernels for 0%

profile of v1, /device:TPU:1, one launch (start us, length us, event | category | flops | bytes accessed | tf_op | source)
XLA Modules:
  0.0 1357.0 jit_solution(1884577453902209824)
XLA Ops:
  22.9 44.0 %all-gather.20.cloned.1.call-done = bf16[576,3456]{1,0:T(8,128)(2,1)} async-done(((bf16[288,3456]{1,0:T(8,128)(2,1)}), bf16[576,3456]{1,0:T(8,128)(2,1)}) %all-gather.20.cloned.1.call-update) | async-done | bytes 3981328 | tf_op jit(solution)/shard_map/all_gather | solution.py:57
  67.6 4.4 fusion.59
  72.0 6.0 psum.56
  84.5 5.1 convert_reduce_fusion.2
  89.6 49.3 %all-gather.26.cloned.1.call-done = bf16[2304,1152]{1,0:T(8,128)(2,1)} async-done(((bf16[1152,1152]{1,0:T(8,128)(2,1)}), bf16[2304,1152]{1,0:T(8,128)(2,1)}) %all-gather.26.cloned.1.call-update) | async-done | bytes 5308432 | tf_op jit(solution)/shard_map/all_gather | solution.py:57
  139.6 5.0 select_bitcast_fusion.5
  144.6 6.3 pad_maximum_fusion.2
  150.9 12.3 fusion.60
  163.2 5.3 copy-done.8
  176.3 60.5 %all-gather.24.cloned.1.call-done = bf16[576,4608]{1,0:T(8,128)(2,1)} async-done(((bf16[288,4608]{1,0:T(8,128)(2,1)}), bf16[576,4608]{1,0:T(8,128)(2,1)}) %all-gather.24.cloned.1.call-update) | async-done | bytes 5308432 | tf_op jit(solution)/shard_map/all_gather | solution.py:57
  239.3 6.8 fusion.40
  246.1 9.6 reshape.308
  255.8 7.1 copy.62
  263.0 9.2 select_bitcast_fusion.1
  272.2 9.9 pad_maximum_fusion.1
  282.1 8.9 select_bitcast_fusion.3
  291.0 9.3 pad_maximum_fusion
  300.9 6.6 copy.61
  307.6 27.5 %multiply_reduce_fusion = (f32[2,16,512]{2,1,0:T(8,128)S(1)}, f32[2,16,512,1024]{3,2,1,0:T(8,128)}) fusion(bf16[2,512,16,72]{1,3,2,0:T(8,128)(2,1)} %copy.62, bf16[2,1024,16,72]{1,3,2,0:T(8,128)(2,1)} %bitcast.194), kind=kOutput, calls=%fused_computation.4 | convolution fusion | flops 2449457152 | bytes 74252288 | tf_op jit(solution)/shard_map/sqhd,skhd->shqk/dot_general | solution.py:153
  335.0 21.3 %exponential_reduce_fusion = f32[2,16,512]{2,1,0:T(8,128)S(1)} fusion(f32[2,16,512,1024]{3,2,1,0:T(8,128)} %get-tuple-element.71, f32[2,16,512]{2,1,0:T(8,128)S(1)} %get-tuple-element.70), kind=kLoop, calls=%fused_computation.2 | loop fusion | flops 50315264 | bytes 67239936 | tf_op jit(solution)/shard_map/reduce_sum | solution.py:156
  356.4 8.6 all-gather.16.cloned.1.call-done
  365.0 6.6 copy.59
  371.6 28.2 %bitcast_convert_fusion.2 = (bf16[2,512,16,72]{1,3,2,0:T(8,128)(2,1)}, f32[2,16,72,512]{3,2,1,0:T(8,128)}) fusion(bf16[2,1024,16,72]{1,3,2,0:T(8,128)(2,1)} %bitcast.192, f32[2,16,512,1024]{3,2,1,0:T(8,128)} %get-tuple-element.71, f32[2,16,512]{2,1,0:T(8,128)S(1)} %log_add_fusion), kind=kOutput, calls=%fused_computation.77 | convolution fusion | flops 2467430400 | bytes 78970880 | tf_op jit(solution)/shard_map/shqk,skhd->sqhd/dot_general | solution.py:158
  416.2 15.4 %fusion.61 = f32[1024,4608]{1,0:T(8,128)} fusion(bf16[1024,1152]{1,0:T(8,128)(2,1)S(1)} %bitcast.238, bf16[1152,4608]{1,0:T(8,128)(2,1)S(1)} %bitcast.210), kind=kOutput, calls=%fused_computation.179 | convolution fusion | flops 10871635968 | bytes 31850496 | tf_op jit(solution)/shard_map/dot_general | solution.py:33
  431.6 22.7 %convolution_convert_fusion = bf16[4608,1152]{1,0:T(8,128)(2,1)} fusion(bf16[1024,1152]{1,0:T(8,128)(2,1)S(1)} %bitcast.236, f32[1024,4608]{1,0:T(8,128)} %fusion.61, f32[4608]{0:T(1024)S(1)} %reshape.282), kind=kOutput, calls=%fused_computation.7 | convolution fusion | flops 10924130304 | bytes 31868928 | tf_op jit(solution)/shard_map/dot_general | solution.py:64
  454.3 5.2 dynamic-slice_bitcast_fusion
  460.2 29.3 %convert_reduce_fusion = (f32[4608]{0:T(1024)}, bf16[1024,4608]{1,0:T(8,128)(2,1)}) fusion(f32[1024,4608]{1,0:T(8,128)} %fusion.61, f32[4608]{0:T(1024)S(1)} %reshape.282, bf16[1024,1152]{1,0:T(8,128)(2,1)S(1)} %bitcast.237, bf16[4608,1152]{1,0:T(8,128)(2,1)} %bitcast.205), kind=kOutput, calls=%fused_computation.16 | convolution fusion | flops 10980159488 | bytes 41324544 | tf_op jit(solution)/shard_map/dot_general | solution.py:26
  489.5 21.3 %multiply_reduce_fusion.2 = (f32[2,1152]{1,0:T(2,128)}, f32[2,512]{1,0:T(2,128)S(1)}, f32[2,512]{1,0:T(2,128)S(1)}, f32[2,1152]{1,0:T(2,128)}, f32[2,512,1152]{2,1,0:T(8,128)}) fusion(f32[2,512,1152]{2,1,0:T(8,128)} %copy-done.2, f32[2,512]{1,0:T(2,128)S(1)} %add_rsqrt_fusion, f32[2,512]{1,0:T(2,128)S(1)} %broadcast_multiply_fusion.4, ...), kind=kOutput, calls=%fused_computation.84 | convolution fusion | flops 10882246656 | bytes 29535232 | tf_op jit(solution)/shard_map/dot_general | solution.py:26
  510.8 7.7 fusion.8
  519.3 21.8 %convolution_add_fusion = f32[1024,1152]{1,0:T(8,128)S(1)} fusion(bf16[4608,1152]{1,0:T(8,128)(2,1)} %bitcast.206, f32[1152]{0:T(1024)S(1)} %copy-done.47, f32[1024,4608]{1,0:T(8,128)} %fusion.61, f32[4608]{0:T(1024)S(1)} %reshape.282), kind=kOutput, calls=%fused_computation.62 | convolution fusion | flops 10920001536 | bytes 34232832 | tf_op jit(solution)/shard_map/dot_general | solution.py:33
  541.1 8.8 convert_reduce_fusion.3
  551.4 4.8 convolution_convert_fusion.4
  556.2 9.6 reshape.309
  565.8 7.1 copy.68
  577.0 40.1 %multiply_convert_fusion = bf16[2,16,512,1024]{3,2,1,0:T(8,128)(2,1)} fusion(f32[2,16,512,1024]{3,2,1,0:T(8,128)} %get-tuple-element.71, f32[2,16,512]{2,1,0:T(8,128)S(1)} %bitcast.247, f32[2,16,512]{2,1,0:T(8,128)S(1)} %copy-done.12, bf16[2,512,16,72]{1,3,2,0:T(8,128)(2,1)S(1)} %copy-done.5, bf16[2,1024,16,72]{1,3,2,0:T(8,128)(2,1)} %bitcast.193), kind=kOutput, calls=%fused_computation | convolution fusion | flops 2499805184 | bytes 107872256 | tf_op jit(solution)/shard_map/sqhd,skhd->shqk/dot_general | solution.py:201
  617.1 19.4 %multiply_convert_fusion.2 = bf16[2,16,72,1024]{3,2,1,0:T(8,128)(2,1)} fusion(bf16[2,512,16,72]{1,3,2,0:T(8,128)(2,1)} %copy.62, bf16[2,16,512,1024]{3,2,1,0:T(8,128)(2,1)} %multiply_convert_fusion), kind=kOutput, calls=%fused_computation.25 | convolution fusion | flops 2420637696 | bytes 40632320 | tf_op jit(solution)/shard_map/shqk,sqhd->skhd/dot_general | solution.py:216
  636.6 6.7 copy.71
  643.4 28.0 %fusion.43 = bf16[2,16,72,1024]{3,2,1,0:T(8,128)(2,1)} fusion(bf16[2,512,16,72]{1,3,2,0:T(8,128)(2,1)} %copy.68, f32[2,16,512,1024]{3,2,1,0:T(8,128)} %get-tuple-element.71, f32[2,16,512]{2,1,0:T(8,128)S(1)} %copy-done.12), kind=kOutput, calls=%fused_computation.105 | convolution fusion | flops 2468610048 | bytes 74252288 | tf_op jit(solution)/shard_map/shqk,sqhd->skhd/dot_general | solution.py:221
  671.4 6.7 copy.73
  678.2 14.8 %convolution_convert_fusion.1 = bf16[1152,4608]{1,0:T(8,128)(2,1)S(1)} fusion(bf16[1024,1152]{1,0:T(8,128)(2,1)} %bitcast.239, bf16[1024,4608]{1,0:T(8,128)(2,1)} %get-tuple-element.32), kind=kOutput, calls=%fused_computation.8 | convolution fusion | flops 10876944384 | bytes 22413312 | tf_op jit(solution)/shard_map/dot_general | solution.py:64
  693.4 8.9 collective-permute-done.6
  702.3 6.2 fusion.9
  708.6 5.6 convolution_convert_fusion.3
  716.1 18.1 %convert_reduce_fusion.5 = (f32[16,72]{1,0:T(8,128)S(1)}, bf16[2,16,72,512]{3,2,1,0:T(8,128)(2,1)S(1)}) fusion(bf16[2,1024,16,72]{1,3,2,0:T(8,128)(2,1)} %bitcast.195, bf16[2,16,512,1024]{3,2,1,0:T(8,128)(2,1)} %multiply_convert_fusion), kind=kOutput, calls=%fused_computation.82 | convolution fusion | flops 2420636672 | bytes 40636928 | tf_op jit(solution)/shard_map/shqk,skhd->sqhd/dot_general | solution.py:209
  744.6 20.7 %reduce-scatter.9.cloned.1.call-done = bf16[2,512,1152]{2,1,0:T(8,128)(2,1)} async-done(((bf16[2,1024,1152]{2,1,0:T(8,128)(2,1)}), bf16[2,512,1152]{2,1,0:T(8,128)(2,1)}) %reduce-scatter.9.cloned.1.call-update) | async-done | bytes 2359312 | tf_op jit(solution)/shard_map/reduce_scatter | solution.py:231
  769.6 12.2 convolution_convert_fusion.2
  787.9 46.5 %reduce-scatter.15.cloned.1.call-done = bf16[1,288,4608]{2,1,0:T(8,128)(2,1)} async-done(((bf16[2,288,4608]{2,1,0:T(8,128)(2,1)}), bf16[1,288,4608]{2,1,0:T(8,128)(2,1)}) %reduce-scatter.15.cloned.1.call-update) | async-done | bytes 2654224 | tf_op jit(solution)/shard_map/reduce_scatter | solution.py:74
  834.4 118.8 %all-reduce.5.cloned.1.call-done = bf16[1152,1152]{1,0:T(8,128)(2,1)} async-done(((bf16[1152,1152]{1,0:T(8,128)(2,1)}), bf16[1152,1152]{1,0:T(8,128)(2,1)}) %all-reduce.5.cloned.1.call-update) | async-done | bytes 2654224 | tf_op jit(solution)/shard_map/psum | solution.py:78
  953.3 21.4 %all-gather.7 = bf16[16,2,576]{2,1,0:T(2,128)(2,1)S(1)} all-gather(bf16[1,2,576]{2,1,0:T(2,128)(2,1)S(1)} %bitcast.254), channel_id=1, replica_groups=mesh['chip'=8,'core'=2,'shard'=2] {'chip','core'}, dimensions={0}, use_global_device_ids=true | all-gather | bytes 39168 | tf_op jit(solution)/shard_map/all_gather | solution.py:250
  974.8 4.3 copy.74
  981.2 6.2 fusion.10
  987.7 17.0 %fusion.38 = (f32[2,1152]{1,0:T(2,128)S(1)}, f32[2,512]{1,0:T(2,128)S(1)}, f32[2,512]{1,0:T(2,128)S(1)}, f32[2,1152]{1,0:T(2,128)S(1)}, f32[2,512,1152]{2,1,0:T(8,128)}) fusion(bf16[2,512,1152]{2,1,0:T(8,128)(2,1)} %param.14, f32[2,512]{1,0:T(2,128)S(1)} %copy-done.38, f32[2,512]{1,0:T(2,128)S(1)} %copy-done.32, f32[2,1152]{1,0:T(2,128)S(1)} %copy-done.30, ...), kind=kOutput, calls=%fused_computation.69 | convolution fusion | flops 8186750976 | bytes 22162432 | tf_op jit(solution)/shard_map/dot_general | solution.py:26
  1004.8 8.0 multiply_reduce_fusion.3
  1012.9 13.1 psum.62
  1025.9 26.8 %psum.63 = f32[9216]{0:T(1024)S(1)} all-reduce(f32[9216]{0:T(1024)S(1)} %psum.62), channel_id=1, replica_groups=mesh['chip'=8,'core'=2,'shard'=2] {'chip'}, use_global_device_ids=true, to_apply=%region_36.37 | all-reduce | flops 9216 | bytes 73728 | tf_op jit(solution)/shard_map/psum | solution.py:261
  1054.1 7.2 psum.57
  1061.4 5.4 convolution_bitcast_fusion
  1070.1 32.9 %all-gather.8 = bf16[16,2,6912]{2,1,0:T(2,128)(2,1)S(1)} all-gather(bf16[1,2,6912]{2,1,0:T(2,128)(2,1)S(1)} %bitcast.249), channel_id=1, replica_groups=mesh['chip'=8,'core'=2,'shard'=2] {'chip','core'}, dimensions={0}, use_global_device_ids=true | all-gather | bytes 470016 | tf_op jit(solution)/shard_map/all_gather | solution.py:251
  1105.3 8.2 fusion.62
  1119.9 36.3 %reduce-scatter.11.cloned.1.call-done = bf16[1,288,3456]{2,1,0:T(8,128)(2,1)} async-done(((bf16[2,288,3456]{2,1,0:T(8,128)(2,1)}), bf16[1,288,3456]{2,1,0:T(8,128)(2,1)}) %reduce-scatter.11.cloned.1.call-update) | async-done | bytes 1990672 | tf_op jit(solution)/shard_map/reduce_scatter | solution.py:74
  1156.2 75.7 %all-reduce.9.cloned.1.call-done = bf16[288,1152]{1,0:T(8,128)(2,1)} async-done(((bf16[288,1152]{1,0:T(8,128)(2,1)}), bf16[288,1152]{1,0:T(8,128)(2,1)}) %all-reduce.9.cloned.1.call-update) | async-done | bytes 663568 | tf_op jit(solution)/shard_map/psum | solution.py:78
  1234.1 7.3 bitcast_convert_fusion
  1243.4 91.8 %all-reduce.11.cloned.1.call-done = bf16[288,3456]{1,0:T(8,128)(2,1)} async-done(((bf16[288,3456]{1,0:T(8,128)(2,1)}), bf16[288,3456]{1,0:T(8,128)(2,1)}) %all-reduce.11.cloned.1.call-update) | async-done | bytes 1990672 | tf_op jit(solution)/shard_map/psum | solution.py:78
  1339.5 5.9 bitcast_convert_fusion.1
  (262 shorter events, 109.0 us)
Async XLA Ops:
  7.2 6.8 copy-start
  7.2 59.7 %all-gather.20.cloned.1.call-start = ((), (), s32[]{:S(2)}) async-start(), calls=%async_computation.18 | async-start | bytes 5971968 | tf_op jit(solution)/shard_map/all_gather | solution.py:57
  10.3 128.6 %all-gather.26.cloned.1.call-start = ((), (), s32[]{:S(2)}) async-start(), calls=%async_computation.21 | async-start | bytes 7962624 | tf_op jit(solution)/shard_map/all_gather | solution.py:57
  14.0 156.6 %all-gather.22.cloned.1.call-start = ((), (), s32[]{:S(2)}) async-start(), calls=%async_computation.19 | async-start | bytes 1990656 | tf_op jit(solution)/shard_map/all_gather | solution.py:57
  14.9 221.9 %all-gather.24.cloned.1.call-start = ((), (), s32[]{:S(2)}) async-start(), calls=%async_computation.20 | async-start | bytes 7962624 | tf_op jit(solution)/shard_map/all_gather | solution.py:57
  18.4 282.5 %all-gather.18.cloned.1.call-start = ((), (), s32[]{:S(2)}) async-start(), calls=%async_computation.7 | async-start | bytes 7077888 | tf_op jit(solution)/shard_map/all_gather | solution.py:146
  22.9 44.7 %copy-start.39 = (bf16[2,576]{1,0:T(2,128)(2,1)}, bf16[2,576]{1,0:T(2,128)(2,1)S(1)}, u32[]{:S(2)}) copy-start(bf16[2,576]{1,0:T(2,128)(2,1)S(1)} %fusion.50) | copy-start | bytes 6916
  66.9 72.7 %collective-permute-start = (bf16[2,288,3456]{2,1,0:T(8,128)(2,1)}, bf16[2,288,3456]{2,1,0:T(8,128)(2,1)}, u32[]{:S(2)}, u32[]{:S(2)}) collective-permute-start(bf16[2,288,3456]{2,1,0:T(8,128)(2,1)} %bitcast.224), channel_id=1, source_target_pairs={{0,2},{2,0},{1,3},{3,1},{4,6},{6,4},{5,7},{7,5},{8,10},{10,8},{9,1... | collective-permute-start | bytes 11943944 | tf_op jit(solution)/shard_map/ppermute | solution.py:43
  80.6 9.0 copy-start.31
  83.9 5.7 copy-start.50
  83.9 5.7 copy-start.37
  84.5 5.1 copy-start.24
  84.5 5.1 copy-start.29
  84.5 323.9 %copy-start.27 = (f32[2,1152]{1,0:T(2,128)}, f32[2,1152]{1,0:T(2,128)S(1)}, u32[]{:S(2)}) copy-start(f32[2,1152]{1,0:T(2,128)S(1)} %get-tuple-element.65) | copy-start | bytes 27652
  138.9 124.0 %collective-permute-start.3 = (bf16[2,1152,1152]{2,1,0:T(8,128)(2,1)}, bf16[2,1152,1152]{2,1,0:T(8,128)(2,1)}, u32[]{:S(2)}, u32[]{:S(2)}) collective-permute-start(bf16[2,1152,1152]{2,1,0:T(8,128)(2,1)} %bitcast.220), channel_id=1, source_target_pairs={{0,2},{2,0},{1,3},{3,1},{4,6},{6,4},{5,7},{7,5},{8,10},{10,8},{9,1... | collective-permute-start | bytes 15925256 | tf_op jit(solution)/shard_map/ppermute | solution.py:43
  144.6 6.3 copy-start.18
  163.2 5.3 copy-start.8
  170.3 194.7 %all-gather.16.cloned.1.call-start = ((), (), s32[]{:S(2)}) async-start(), calls=%async_computation.6 | async-start | bytes 7077888 | tf_op jit(solution)/shard_map/all_gather | solution.py:147
  170.5 3.5 collective-permute-start.1
  236.9 45.2 %collective-permute-start.2 = (bf16[2,288,4608]{2,1,0:T(8,128)(2,1)}, bf16[2,288,4608]{2,1,0:T(8,128)(2,1)}, u32[]{:S(2)}, u32[]{:S(2)}) collective-permute-start(bf16[2,288,4608]{2,1,0:T(8,128)(2,1)} %bitcast.222), channel_id=1, source_target_pairs={{0,2},{2,0},{1,3},{3,1},{4,6},{6,4},{5,7},{7,5},{8,10},{10,8},{9,1... | collective-permute-start | bytes 15925256 | tf_op jit(solution)/shard_map/ppermute | solution.py:43
  262.9 453.1 %reduce-scatter.17.cloned.1.call-start = ((), (), s32[]{:S(2)}) async-start(), calls=%async_computation.13 | async-start | bytes 7962624 | tf_op jit(solution)/shard_map/reduce_scatter | solution.py:74
  356.4 15.3 %copy-start.11 = (f32[2,16,512]{2,1,0:T(8,128)}, f32[2,16,512]{2,1,0:T(8,128)S(1)}, u32[]{:S(2)}) copy-start(f32[2,16,512]{2,1,0:T(8,128)S(1)} %log_add_fusion) | copy-start | bytes 196612
  399.8 4.9 copy-start.13
  408.5 6.4 slice-start
  408.5 6.4 slice-start.1
  410.8 5.4 slice-start.2
  414.9 16.7 %copy-start.20 = (bf16[2,512,1152]{2,1,0:T(8,128)(2,1)}, bf16[2,512,1152]{2,1,0:T(8,128)(2,1)S(1)}, u32[]{:S(2)}) copy-start(bf16[2,512,1152]{2,1,0:T(8,128)(2,1)S(1)} %add_convert_fusion) | copy-start | bytes 7077892
  416.2 15.4 %copy-start.19 = (bf16[2,512,1152]{2,1,0:T(8,128)(2,1)S(1)}, bf16[2,512,1152]{2,1,0:T(8,128)(2,1)}, u32[]{:S(2)}) copy-start(bf16[2,512,1152]{2,1,0:T(8,128)(2,1)} %get-tuple-element.30) | copy-start | bytes 7077892
  459.5 51.3 %collective-permute-start.7 = (bf16[2,1152,1152]{2,1,0:T(8,128)(2,1)}, bf16[2,1152,1152]{2,1,0:T(8,128)(2,1)}, u32[]{:S(2)}, u32[]{:S(2)}) collective-permute-start(bf16[2,1152,1152]{2,1,0:T(8,128)(2,1)} %dynamic-slice_bitcast_fusion), channel_id=1, source_target_pairs={{0,2},{2,0},{1,3},{3,1},{4,6},{6,4},{5,7},{7,5},{8,10},{10,8},{9,1... | collective-permute-start | bytes 15925256 | tf_op jit(solution)/shard_map/ppermute | solution.py:43
  518.6 22.5 %copy-start.25 = (f32[2,1152]{1,0:T(2,128)S(1)}, f32[2,1152]{1,0:T(2,128)}, u32[]{:S(2)}) copy-start(f32[2,1152]{1,0:T(2,128)} %copy-done.24) | copy-start | bytes 27652
  518.6 22.5 %copy-start.28 = (f32[2,1152]{1,0:T(2,128)S(1)}, f32[2,1152]{1,0:T(2,128)}, u32[]{:S(2)}) copy-start(f32[2,1152]{1,0:T(2,128)} %copy-done.27) | copy-start | bytes 27652
  518.6 22.5 %copy-start.51 = (f32[2]{0:T(128)S(1)}, f32[2]{0:T(128)}, u32[]{:S(2)}) copy-start(f32[2]{0:T(128)} %copy-done.50) | copy-start | bytes 28
  518.6 221.6 %reduce-scatter.7.cloned.1.call-start = ((), (), s32[]{:S(2)}) async-start(), calls=%async_computation.8 | async-start | bytes 7077888 | tf_op jit(solution)/shard_map/reduce_scatter | solution.py:228
  519.3 21.8 %copy-start.9 = (bf16[2,512,1152]{2,1,0:T(8,128)(2,1)S(1)}, bf16[2,512,1152]{2,1,0:T(8,128)(2,1)}, u32[]{:S(2)}) copy-start(bf16[2,512,1152]{2,1,0:T(8,128)(2,1)} %param.16) | copy-start | bytes 7077892
  541.1 10.3 copy-start.14
  643.3 122.0 %reduce-scatter.9.cloned.1.call-start = ((), (), s32[]{:S(2)}) async-start(), calls=%async_computation.9 | async-start | bytes 7077888 | tf_op jit(solution)/shard_map/reduce_scatter | solution.py:231
  678.1 156.3 %reduce-scatter.15.cloned.1.call-start = ((), (), s32[]{:S(2)}) async-start(), calls=%async_computation.12 | async-start | bytes 7962624 | tf_op jit(solution)/shard_map/reduce_scatter | solution.py:74
  693.3 8.9 collective-permute-start.6
  708.5 244.7 %all-reduce.5.cloned.1.call-start = ((), (), s32[]{:S(2)}) async-start(), calls=%async_computation.14 | async-start | bytes 5308416 | tf_op jit(solution)/shard_map/psum | solution.py:78
  715.8 22.9 %collective-permute-start.5 = (bf16[2,288,1152]{2,1,0:T(8,128)(2,1)S(1)}, bf16[2,288,1152]{2,1,0:T(8,128)(2,1)S(1)}, u32[]{:S(2)}, u32[]{:S(2)}) collective-permute-start(bf16[2,288,1152]{2,1,0:T(8,128)(2,1)S(1)} %dynamic-slice_bitcast_fusion.3), channel_id=1, source_target_pairs={{0,2},{2,0},{1,3},{3,1},{4,6},{6,4},{5,7},{7,5},{8,10},{10,8},{9,1... | collective-permute-start | bytes 3981320 | tf_op jit(solution)/shard_map/ppermute | solution.py:43
  716.1 397.4 %reduce-scatter.13.cloned.1.call-start = ((), (), s32[]{:S(2)}) async-start(), calls=%async_computation.11 | async-start | bytes 1990656 | tf_op jit(solution)/shard_map/reduce_scatter | solution.py:74
  740.2 373.3 %all-reduce.7.cloned.1.call-start = ((), (), s32[]{:S(2)}) async-start(), calls=%async_computation.15 | async-start | bytes 5308416 | tf_op jit(solution)/shard_map/psum | solution.py:78
  785.0 168.3 %copy-start.40 = (bf16[2,576]{1,0:T(2,128)(2,1)S(1)}, bf16[2,576]{1,0:T(2,128)(2,1)}, u32[]{:S(2)}) copy-start(bf16[2,576]{1,0:T(2,128)(2,1)} %copy-done.39) | copy-start | bytes 6916
  787.3 194.0 %collective-permute-start.4 = (bf16[2,288,3456]{2,1,0:T(8,128)(2,1)}, bf16[2,288,3456]{2,1,0:T(8,128)(2,1)}, u32[]{:S(2)}, u32[]{:S(2)}) collective-permute-start(bf16[2,288,3456]{2,1,0:T(8,128)(2,1)} %dynamic-slice_bitcast_fusion.2), channel_id=1, source_target_pairs={{0,2},{2,0},{1,3},{3,1},{4,6},{6,4},{5,7},{7,5},{8,10},{10,8},{9,1... | collective-permute-start | bytes 11943944 | tf_op jit(solution)/shard_map/ppermute | solution.py:43
  953.3 202.9 %reduce-scatter.11.cloned.1.call-start = ((), (), s32[]{:S(2)}) async-start(), calls=%async_computation.10 | async-start | bytes 5971968 | tf_op jit(solution)/shard_map/reduce_scatter | solution.py:74
  981.2 6.4 copy-start.41
  981.2 6.4 copy-start.43
  981.2 6.4 copy-start.30
  981.2 6.4 copy-start.32
  981.2 6.4 copy-start.38
  987.5 244.4 %all-reduce.9.cloned.1.call-start = ((), (), s32[]{:S(2)}) async-start(), calls=%async_computation.16 | async-start | bytes 1327104 | tf_op jit(solution)/shard_map/psum | solution.py:78
  987.6 17.1 %copy-start.4 = (bf16[2,512,1152]{2,1,0:T(8,128)(2,1)S(1)}, bf16[2,512,1152]{2,1,0:T(8,128)(2,1)}, u32[]{:S(2)}) copy-start(bf16[2,512,1152]{2,1,0:T(8,128)(2,1)} %param.14) | copy-start | bytes 7077892
  1004.7 8.0 copy-start.45
  1004.7 8.1 copy-start.42
  1004.7 49.4 %copy-start.44 = (f32[2,1152]{1,0:T(2,128)S(1)}, f32[2,1152]{1,0:T(2,128)}, u32[]{:S(2)}) copy-start(f32[2,1152]{1,0:T(2,128)} %get-tuple-element.19) | copy-start | bytes 27652
  1004.8 49.4 %copy-start.35 = (f32[2,1152]{1,0:T(2,128)S(1)}, f32[2,1152]{1,0:T(2,128)}, u32[]{:S(2)}) copy-start(f32[2,1152]{1,0:T(2,128)} %get-tuple-element.57) | copy-start | bytes 27652
  1012.8 101.2 %collective-permute-start.11 = (bf16[1152,1152]{1,0:T(8,128)(2,1)}, bf16[1152,1152]{1,0:T(8,128)(2,1)}, u32[]{:S(2)}, u32[]{:S(2)}) collective-permute-start(bf16[1152,1152]{1,0:T(8,128)(2,1)} %all-reduce.5.cloned.1.call-done), channel_id=1, source_target_pairs={{0,2},{2,0},{1,3},{3,1},{4,6},{6,4},{5,7},{7,5},{8,10},{10,8},{9,1... | collective-permute-start | bytes 7962632 | tf_op jit(solution)/shard_map/ppermute | solution.py:43
  1061.4 43.3 %copy-start.34 = (bf16[2,1152]{1,0:T(2,128)(2,1)S(1)}, bf16[2,1152]{1,0:T(2,128)(2,1)}, u32[]{:S(2)}) copy-start(bf16[2,1152]{1,0:T(2,128)(2,1)} %param.15) | copy-start | bytes 13828
  1113.5 221.7 %all-reduce.11.cloned.1.call-start = ((), (), s32[]{:S(2)}) async-start(), calls=%async_computation.17 | async-start | bytes 3981312 | tf_op jit(solution)/shard_map/psum | solution.py:78
  1113.7 222.4 %collective-permute-start.10 = (bf16[288,4608]{1,0:T(8,128)(2,1)}, bf16[288,4608]{1,0:T(8,128)(2,1)}, u32[]{:S(2)}, u32[]{:S(2)}) collective-permute-start(bf16[288,4608]{1,0:T(8,128)(2,1)} %all-reduce.7.cloned.1.call-done), channel_id=1, source_target_pairs={{0,2},{2,0},{1,3},{3,1},{4,6},{6,4},{5,7},{7,5},{8,10},{10,8},{9,1... | collective-permute-start | bytes 7962632 | tf_op jit(solution)/shard_map/ppermute | solution.py:43
  1232.0 9.4 copy-start.23
  1232.0 9.4 collective-permute-start.9
  1335.2 10.2 collective-permute-start.8
  1339.5 5.9 copy-start.22
  (21 other events, 76.8 us)
Sparse Core Ops, SparseCore 0:
  10.5 56.4 all-gather.19
  69.0 69.8 all-gather.25
  141.1 24.4 all-gather.21
  167.5 69.2 all-gather.23
  238.2 62.6 all-gather.17
  302.3 62.6 all-gather.15
  518.7 65.8 reduce-scatter.16
  643.5 59.3 reduce-scatter.6
  705.3 59.9 reduce-scatter.8
  768.0 66.3 reduce-scatter.14
  838.1 115.0 all-reduce.4
  955.3 23.3 reduce-scatter.12
  982.9 117.7 all-reduce.6
  1103.5 52.6 reduce-scatter.10
  1159.9 72.0 all-reduce.8
  1235.4 99.7 all-reduce.10
